TPU v7x, 32 devices: a whole 2x2x4 slice. The times are simulated.
32 devices in a mesh: groups: 2 (over x), owner: 16 (over z, y, core).
Axes of the slice: x: 2, y: 2, z: 4, core: 2. Of those that a mesh axis runs over, the one named last changes fastest.
Arguments:
- queries: bfloat16 [512, 8192], P(('groups', 'owner')), parts along dimension 0, may hold values from -12 to 12
- request_prefix: int32 [512, 1], P(('groups', 'owner')), parts along dimension 0, may hold values from 0 to 15; in each aligned block of 16 rows (0 to 15, 16 to 31, ...) at most 2 rows name the same one
- suffix_len: int32 [512], P(('groups', 'owner')), parts along dimension 0, may hold values from 1 to 32, 4096 in all
- block_map: int32 [64], P('groups'), parts along dimension 0, may hold values from 0 to 31, each once
- prefix_keys: bfloat16 [64, 1024, 1024], P(('groups', 'owner')), parts along dimension 0, may hold values from -12 to 12
- prefix_values: bfloat16 [64, 1024, 1024], P(('groups', 'owner')), parts along dimension 0, may hold values from -10 to 10
- suffix_keys: bfloat16 [512, 32, 1024], P(('groups', 'owner')), parts along dimension 0, may hold values from -12 to 12
- suffix_values: bfloat16 [512, 32, 1024], P(('groups', 'owner')), parts along dimension 0, may hold values from -10 to 10
Outputs:
- attended: bfloat16 [512, 8192], P(('groups', 'owner')), parts along dimension 0
There are 2 independent parts, one for each index of `groups`. A program takes and returns all parts, laid end to end along the dimension named above; each array names one. Nothing has to cross between parts.
Inputs may be any that keep to these rules, and one draw needn't show every extreme that they name: `request_prefix`: at most 2 requests of one device continue the same prefix. `block_map`: each slot appears once; slot s lies on owner s // 2.
All inputs are finite; a program needn't handle non-finite values. No bound on the sum of `suffix_len` on one device may be relied on, other than what follows from the above.
Results may differ from a plain program's by a relative error of at most 0.0043.
Values may be sent and summed in bfloat16 or wider, within the bound.
No kernel may reach another device: no remote copies, remote signals or barrier semaphores. Data moves between devices by JAX's collectives and lax.ppermute only.
A program may use at most 128 MiB of HBM per device.

v0:
```python
import math

import jax
import jax.numpy as jnp
from jax import lax
from jax.sharding import PartitionSpec as P

HEADS = 64
KV_HEADS = 8
HEAD_DIM = 128
PREFIXES = 16
CAP = 2


NEG_FILL = -1e30


def span_terms(rows, span_keys, span_values):
    row_count = rows.shape[0]
    per_group = HEADS // KV_HEADS
    factor = 1.0 / math.sqrt(HEAD_DIM)
    query_heads = rows.reshape(row_count, KV_HEADS, per_group, HEAD_DIM)
    key_heads = span_keys.reshape(span_keys.shape[0], KV_HEADS, HEAD_DIM)
    value_heads = span_values.reshape(span_values.shape[0], KV_HEADS, HEAD_DIM)
    out_list = []
    lse_list = []
    for kv_head in range(KV_HEADS):
        scores = (
            jnp.einsum(
                "rgd,td->rgt",
                query_heads[:, kv_head],
                key_heads[:, kv_head],
                preferred_element_type=jnp.float32,
            )
            * factor
        )
        highest = jnp.max(scores, axis=-1, keepdims=True)
        expon = jnp.exp(scores - highest)
        summed = jnp.sum(expon, axis=-1)
        weights = expon.astype(jnp.bfloat16)
        mixed = (
            jnp.einsum(
                "rgt,td->rgd", weights, value_heads[:, kv_head], preferred_element_type=jnp.float32
            )
            / summed[..., None]
        )
        out_list.append(mixed.astype(jnp.bfloat16))
        lse_list.append(highest[..., 0] + jnp.log(summed))
    span_out = jnp.stack(out_list, axis=1).reshape(row_count, HEADS * HEAD_DIM)
    span_lse = jnp.stack(lse_list, axis=1).reshape(row_count, HEADS)
    return (span_out, span_lse)


def attend_rows(received, prefix_keys, prefix_values):
    sources, local_slots, item_count, row_width = received.shape
    out_list = []
    lse_list = []
    for slot_index in range(local_slots):
        rows = received[:, slot_index].reshape(sources * item_count, row_width)
        span_out, span_lse = span_terms(rows, prefix_keys[slot_index], prefix_values[slot_index])
        out_list.append(span_out.reshape(sources, item_count, row_width))
        lse_list.append(span_lse.reshape(sources, item_count, HEADS))
    return (jnp.stack(out_list, axis=1), jnp.stack(lse_list, axis=1))


def suffix_terms(queries, suffix_keys, suffix_values, suffix_len):
    row_count = queries.shape[0]
    suffix_room = suffix_keys.shape[1]
    per_group = HEADS // KV_HEADS
    factor = 1.0 / math.sqrt(HEAD_DIM)
    query_heads = queries.reshape(row_count, KV_HEADS, per_group, HEAD_DIM)
    key_heads = suffix_keys.reshape(row_count, suffix_room, KV_HEADS, HEAD_DIM)
    value_heads = suffix_values.reshape(row_count, suffix_room, KV_HEADS, HEAD_DIM)
    scores = (
        jnp.einsum("rhgd,rthd->rhgt", query_heads, key_heads, preferred_element_type=jnp.float32)
        * factor
    )
    visible = (jnp.arange(suffix_room, dtype=jnp.int32)[None, :] < suffix_len[:, None])[
        :, None, None, :
    ]
    highest = jnp.max(jnp.where(visible, scores, NEG_FILL), axis=-1, keepdims=True)
    expon = jnp.where(visible, jnp.exp(scores - highest), 0.0)
    summed = jnp.sum(expon, axis=-1)
    weights = expon.astype(jnp.bfloat16)
    mixed = (
        jnp.einsum("rhgt,rthd->rhgd", weights, value_heads, preferred_element_type=jnp.float32)
        / summed[..., None]
    )
    suffix_out = mixed.reshape(row_count, HEADS, HEAD_DIM)
    suffix_lse = (highest[..., 0] + jnp.log(summed)).reshape(row_count, HEADS)
    return (suffix_out, suffix_lse)


def combine_terms(span_out, span_lse, suffix_out, suffix_lse):
    row_count = span_out.shape[0]
    highest = jnp.maximum(jnp.max(span_lse, axis=1), suffix_lse)
    span_scale = jnp.exp(span_lse - highest[:, None, :])
    suffix_scale = jnp.exp(suffix_lse - highest)
    numerator = (
        jnp.sum(span_scale[..., None] * span_out.astype(jnp.float32), axis=1)
        + suffix_scale[..., None] * suffix_out
    )
    denominator = jnp.sum(span_scale, axis=1) + suffix_scale
    return (
        (numerator / denominator[..., None])
        .astype(jnp.bfloat16)
        .reshape(row_count, HEADS * HEAD_DIM)
    )


def body(
    queries,
    request_prefix,
    suffix_len,
    block_map,
    prefix_keys,
    prefix_values,
    suffix_keys,
    suffix_values,
):
    owners = lax.axis_size("owner")
    local_rows = queries.shape[0]
    row_width = queries.shape[1]
    slot_count = block_map.shape[0]
    local_slots = prefix_keys.shape[0]
    per_prefix = slot_count // PREFIXES
    slot_range = jnp.arange(slot_count, dtype=jnp.int32)
    prefix_ids = request_prefix[:, 0]
    span_ids = prefix_ids[:, None] * per_prefix + jnp.arange(per_prefix, dtype=jnp.int32)[None, :]
    table_match = span_ids[:, :, None] == slot_range[None, None, :]
    slot_of = jnp.sum(jnp.where(table_match, block_map[None, None, :], 0), axis=-1)
    row_order = jnp.arange(local_rows, dtype=jnp.int32)
    earlier = (prefix_ids[:, None] == prefix_ids[None, :]) & (
        row_order[None, :] < row_order[:, None]
    )
    row_rank = jnp.sum(earlier.astype(jnp.int32), axis=1)
    position = slot_of * CAP + row_rank[:, None]
    buffer_match = (
        position[:, :, None] == jnp.arange(slot_count * CAP, dtype=jnp.int32)[None, None, :]
    )
    picker = jnp.any(buffer_match, axis=1).astype(jnp.bfloat16)
    outgoing = jnp.einsum("ib,id->bd", picker, queries, preferred_element_type=jnp.float32).astype(
        jnp.bfloat16
    )
    outgoing = outgoing.reshape(owners, local_slots, CAP, row_width)
    part_out, part_lse = attend_rows(
        lax.all_to_all(outgoing, "owner", split_axis=0, concat_axis=0, tiled=True),
        prefix_keys,
        prefix_values,
    )
    back_out = lax.all_to_all(part_out, "owner", split_axis=0, concat_axis=0, tiled=True)
    back_lse = lax.all_to_all(part_lse, "owner", split_axis=0, concat_axis=0, tiled=True)
    flat_out = back_out.reshape(slot_count * CAP, row_width)
    flat_lse = back_lse.reshape(slot_count * CAP, HEADS)
    flat_index = position.reshape(-1)
    span_out = jnp.take(flat_out, flat_index, axis=0).reshape(
        local_rows, per_prefix, HEADS, HEAD_DIM
    )
    span_lse = jnp.take(flat_lse, flat_index, axis=0).reshape(local_rows, per_prefix, HEADS)
    suffix_out, suffix_lse = suffix_terms(queries, suffix_keys, suffix_values, suffix_len)
    return combine_terms(span_out, span_lse, suffix_out, suffix_lse)


def solution(mesh):
    placed = (
        P(("groups", "owner"), None),
        P(("groups", "owner"), None),
        P(("groups", "owner")),
        P("groups"),
        P(("groups", "owner"), None, None),
        P(("groups", "owner"), None, None),
        P(("groups", "owner"), None, None),
        P(("groups", "owner"), None, None),
    )
    return jax.shard_map(
        body, mesh=mesh, in_specs=placed, out_specs=P(("groups", "owner"), None), check_vma=False
    )
```

profile of v0, /device:TPU:9, one launch (start us, length us, event | category | flops | bytes accessed | tf_op | source)
XLA Modules:
  0.0 133.6 jit_solution(5191109495947289585)
XLA Ops:
  5.5 6.6 %all-to-all-start = ((bf16[16,2,2,8192]{3,2,1,0:T(2,128)(2,1)}), bf16[16,2,2,8192]{3,2,1,0:T(2,128)(2,1)}, u32[]{:S(2)}, u32[]{:S(2)}) async-start(bf16[16,2,2,8192]{3,2,1,0:T(2,128)(2,1)} %reshape.484), calls=%async_computation | async-start | bytes 2097152 | tf_op jit(solution)/shard_map/all_to_all | solution.py:147
  12.2 4.0 %fusion.132 = (bf16[1,1024,1024]{2,1,0:T(8,128)(2,1)S(1)}, bf16[1,1024,1024]{2,1,0:T(8,128)(2,1)}) fusion(bf16[2,1024,1024]{2,1,0:T(8,128)(2,1)} %param.12), kind=kLoop, calls=%fused_computation.256 | loop fusion | bytes 8388608 | tf_op jit(solution)/shard_map/slice | solution.py:60
  16.2 2.6 %copy.316 = bf16[1,1024,1024]{1,2,0:T(8,128)(2,1)} copy(bf16[1,1024,1024]{2,1,0:T(8,128)(2,1)S(1)} %get-tuple-element.13) | data formatting | bytes 4194304
  18.8 4.0 %fusion.131 = (bf16[1,1024,1024]{2,1,0:T(8,128)(2,1)S(1)}, bf16[1,1024,1024]{2,1,0:T(8,128)(2,1)}) fusion(bf16[2,1024,1024]{2,1,0:T(8,128)(2,1)} %param.13), kind=kLoop, calls=%fused_computation.255 | loop fusion | bytes 8388608 | tf_op jit(solution)/shard_map/slice | solution.py:60
  22.8 2.6 %copy.349 = bf16[1,1024,1024]{1,2,0:T(8,128)(2,1)} copy(bf16[1,1024,1024]{2,1,0:T(8,128)(2,1)S(1)} %get-tuple-element.11) | data formatting | bytes 4194304
  25.4 2.9 %copy.333 = bf16[1,1024,1024]{1,2,0:T(8,128)(2,1)S(1)} copy(bf16[1,1024,1024]{2,1,0:T(8,128)(2,1)} %get-tuple-element.14) | data formatting | bytes 4194304
  28.2 4.0 %copy.358 = bf16[1,1024,1024]{1,2,0:T(8,128)(2,1)} copy(bf16[1,1024,1024]{2,1,0:T(8,128)(2,1)} %get-tuple-element.12) | data formatting | bytes 4194304
  34.3 2.8 %all-to-all-done = bf16[16,2,2,8192]{3,2,1,0:T(2,128)(2,1)} async-done(((bf16[16,2,2,8192]{3,2,1,0:T(2,128)(2,1)}), bf16[16,2,2,8192]{3,2,1,0:T(2,128)(2,1)}, u32[]{:S(2)}, u32[]{:S(2)}) %all-to-all-start) | async-done | bytes 1048608 | tf_op jit(solution)/shard_map/all_to_all | solution.py:147
  37.1 3.5 %fusion.133 = (bf16[16,1,2,8192]{3,2,1,0:T(2,128)(2,1)}, bf16[16,1,2,8192]{3,2,1,0:T(2,128)(2,1)}) fusion(bf16[16,2,2,8192]{3,2,1,0:T(2,128)(2,1)} %all-to-all-done), kind=kLoop, calls=%fused_computation.257 | loop fusion | bytes 2097152 | tf_op jit(solution)/shard_map/slice | solution.py:59
  40.6 2.2 %reshape_reshape_squeeze.6 = bf16[32,8,8,128]{3,2,1,0:T(8,128)(2,1)} reshape(bf16[16,1,2,8192]{3,2,1,0:T(2,128)(2,1)} %get-tuple-element.15) | data formatting | bytes 1048576 | tf_op jit(solution)/shard_map/reshape;reshape;squeeze | solution.py:22
  42.8 2.4 %fusion.142 = (f32[32,8]{1,0:T(8,128)S(1)}, f32[32,8,1024]{2,1,0:T(8,128)}) fusion(bf16[1024,8,128]{0,2,1:T(8,128)(2,1)} %bitcast.468, bf16[32,8,8,128]{3,2,1,0:T(8,128)(2,1)} %reshape_reshape_squeeze.6), kind=kOutput, calls=%fused_computation.266 | convolution fusion | flops 67632896 | bytes 1377280 | tf_op jit(solution)/shard_map/rgd,td->rgt/dot_general | solution.py:29
  45.2 2.3 %fusion.143 = (f32[32,8]{1,0:T(8,128)S(1)}, f32[32,8,1024]{2,1,0:T(8,128)}) fusion(bf16[1024,8,128]{0,2,1:T(8,128)(2,1)} %bitcast.469, bf16[32,8,8,128]{3,2,1,0:T(8,128)(2,1)} %reshape_reshape_squeeze.6), kind=kOutput, calls=%fused_computation.267 | convolution fusion | flops 67632896 | bytes 1377280 | tf_op jit(solution)/shard_map/rgd,td->rgt/dot_general | solution.py:29
  55.3 2.3 %reshape_reshape_squeeze.7 = bf16[32,8,8,128]{3,2,1,0:T(8,128)(2,1)} reshape(bf16[16,1,2,8192]{3,2,1,0:T(2,128)(2,1)} %get-tuple-element.16) | data formatting | bytes 1048576 | tf_op jit(solution)/shard_map/reshape;reshape;squeeze | solution.py:22
  57.5 2.2 %fusion.134 = (f32[32,8]{1,0:T(8,128)S(1)}, f32[32,8,1024]{2,1,0:T(8,128)}) fusion(bf16[1024,8,128]{0,2,1:T(8,128)(2,1)S(1)} %bitcast.460, bf16[32,8,8,128]{3,2,1,0:T(8,128)(2,1)} %reshape_reshape_squeeze.7), kind=kOutput, calls=%fused_computation.258 | convolution fusion | flops 67632896 | bytes 1377280 | tf_op jit(solution)/shard_map/rgd,td->rgt/dot_general | solution.py:29
  59.7 2.7 %fusion.135 = (f32[32,8]{1,0:T(8,128)}, f32[32,8,1024]{2,1,0:T(8,128)}) fusion(bf16[1024,8,128]{0,2,1:T(8,128)(2,1)S(1)} %bitcast.461, bf16[32,8,8,128]{3,2,1,0:T(8,128)(2,1)} %reshape_reshape_squeeze.7), kind=kOutput, calls=%fused_computation.259 | convolution fusion | flops 67632896 | bytes 1377280 | tf_op jit(solution)/shard_map/rgd,td->rgt/dot_general | solution.py:29
  77.5 2.0 %stack_reshape_reshape.14 = bf16[16,1,2,8192]{3,2,0,1:T(2,128)(2,1)} reshape(bf16[32,8,8,128]{3,2,1,0:T(8,128)(2,1)} %copy.301) | data formatting | bytes 1048576 | tf_op jit(solution)/shard_map/stack;reshape;reshape | solution.py:63
  80.7 1.6 %fusion.31 = bf16[32,8,8,128]{3,2,0,1:T(8,128)(2,1)S(1)} fusion(f32[32,8,1024]{2,1,0:T(8,128)S(1)} %copy-done.9, f32[32,8]{1,0:T(8,128)} %copy-done.36, bf16[1024,8,128]{0,2,1:T(8,128)(2,1)} %bitcast.477, f32[32,8]{1,0:T(8,128)S(1)} %fusion.69), kind=kOutput, calls=%fused_computation.68 | convolution fusion | flops 67698688 | bytes 1393664 | tf_op jit(solution)/shard_map/rgt,td->rgd/dot_general | solution.py:42
  89.7 4.8 %all-to-all-start.1 = ((f32[16,1,256]{2,1,0:T(1,128)}), f32[16,1,256]{2,1,0:T(1,128)S(1)}, u32[]{:S(2)}, u32[]{:S(2)}) async-start(f32[16,1,256]{2,1,0:T(1,128)} %reshape.539), calls=%async_computation.1 | async-start | bytes 32768 | tf_op jit(solution)/shard_map/all_to_all | solution.py:152
  96.0 1.9 %copy.312 = bf16[16,2,2,8192]{3,2,1,0:T(2,128)(2,1)} copy(bf16[16,2,2,8192]{3,2,0,1:T(2,128)(2,1)S(1)} %pad_maximum_fusion) | data formatting | bytes 2097152 | tf_op jit(solution)/shard_map/stack | solution.py:63
  97.8 1.7 %all-to-all-done.1 = f32[16,1,256]{2,1,0:T(1,128)S(1)} async-done(((f32[16,1,256]{2,1,0:T(1,128)}), f32[16,1,256]{2,1,0:T(1,128)S(1)}, u32[]{:S(2)}, u32[]{:S(2)}) %all-to-all-start.1) | async-done | bytes 16416 | tf_op jit(solution)/shard_map/all_to_all | solution.py:152
  99.5 5.0 %all-to-all-start.2 = ((bf16[16,2,2,8192]{3,2,1,0:T(2,128)(2,1)}), bf16[16,2,2,8192]{3,2,1,0:T(2,128)(2,1)S(1)}, u32[]{:S(2)}, u32[]{:S(2)}) async-start(bf16[16,2,2,8192]{3,2,1,0:T(2,128)(2,1)} %copy.312), calls=%async_computation.2 | async-start | bytes 2097152 | tf_op jit(solution)/shard_map/all_to_all | solution.py:151
  104.6 2.0 %select_reduce_fusion = (f32[16,8,8]{2,1,0:T(8,128)S(1)}, f32[16,8,8,32]{3,2,1,0:T(8,128)S(1)}) fusion(pred[16,32]{1,0:T(8,128)(4,1)S(1)} %iota_compare_fusion.2, bf16[16,8,8,128]{3,2,1,0:T(8,128)(2,1)S(1)} %bitcast.498, bf16[16,32,1024]{2,1,0:T(8,128)(2,1)} %param.14), kind=kOutput, calls=%fused_computation.144 | convolution fusion | flops 8485888 | bytes 1446400 | tf_op jit(solution)/shard_map/rhgd,rthd->rhgt/dot_general | solution.py:75
  110.6 18.9 %all-to-all-done.2 = bf16[16,2,2,8192]{3,2,1,0:T(2,128)(2,1)S(1)} async-done(((bf16[16,2,2,8192]{3,2,1,0:T(2,128)(2,1)}), bf16[16,2,2,8192]{3,2,1,0:T(2,128)(2,1)S(1)}, u32[]{:S(2)}, u32[]{:S(2)}) %all-to-all-start.2) | async-done | bytes 1048608 | tf_op jit(solution)/shard_map/all_to_all | solution.py:151
  131.8 1.8 %fusion.100 = bf16[16,8192]{1,0:T(8,128)(2,1)} fusion(f32[2,8,64,128]{3,2,1,0:T(8,128)S(1)} %bitcast.496, f32[2,8,64,128]{3,2,1,0:T(8,128)S(1)} %bitcast.500, f32[2,8,64,128]{3,2,1,0:T(8,128)S(1)} %bitcast.495, f32[2,8,64,128]{3,2,1,0:T(8,128)S(1)} %bitcast.494), kind=kLoop, calls=%fused_computation.140 | loop fusion | flops 524288 | bytes 2359296 | tf_op jit(solution)/shard_map/convert_element_type | solution.py:106
  (212 shorter events, 46.0 us)
Async XLA Ops:
  0.0 107.2 %copy-start = (bf16[16,32,1024]{2,1,0:T(8,128)(2,1)S(1)}, bf16[16,32,1024]{2,1,0:T(8,128)(2,1)}, u32[]{:S(2)}) copy-start(bf16[16,32,1024]{2,1,0:T(8,128)(2,1)} %param.15) | copy-start | bytes 3145732
  5.5 31.6 %all-to-all-start = ((bf16[16,2,2,8192]{3,2,1,0:T(2,128)(2,1)}), bf16[16,2,2,8192]{3,2,1,0:T(2,128)(2,1)}, u32[]{:S(2)}, u32[]{:S(2)}) async-start(bf16[16,2,2,8192]{3,2,1,0:T(2,128)(2,1)} %reshape.484), calls=%async_computation | async-start | bytes 2097152 | tf_op jit(solution)/shard_map/all_to_all | solution.py:147
  28.2 5.3 %copy-start.23 = (bf16[16,8192]{1,0:T(8,128)(2,1)S(1)}, bf16[16,8192]{1,0:T(8,128)(2,1)}, u32[]{:S(2)}) copy-start(bf16[16,8192]{1,0:T(8,128)(2,1)} %param.8) | copy-start | bytes 786436
  42.8 4.8 %copy-start.1 = (bf16[1,1024,1024]{1,2,0:T(8,128)(2,1)S(1)}, bf16[1,1024,1024]{1,2,0:T(8,128)(2,1)}, u32[]{:S(2)}) copy-start(bf16[1,1024,1024]{1,2,0:T(8,128)(2,1)} %copy.316) | copy-start | bytes 6291460
  42.8 4.8 %copy-start.18 = (bf16[32,8,8,128]{3,2,1,0:T(8,128)(2,1)S(1)}, bf16[32,8,8,128]{3,2,1,0:T(8,128)(2,1)}, u32[]{:S(2)}) copy-start(bf16[32,8,8,128]{3,2,1,0:T(8,128)(2,1)} %reshape_reshape_squeeze.6) | copy-start | bytes 1572868
  47.6 23.7 %copy-start.34 = (f32[32,8]{1,0:T(8,128)}, f32[32,8]{1,0:T(8,128)S(1)}, u32[]{:S(2)}) copy-start(f32[32,8]{1,0:T(8,128)S(1)} %get-tuple-element.35) | copy-start | bytes 3076
  48.9 23.2 %copy-start.32 = (f32[32,8]{1,0:T(8,128)}, f32[32,8]{1,0:T(8,128)S(1)}, u32[]{:S(2)}) copy-start(f32[32,8]{1,0:T(8,128)S(1)} %get-tuple-element.37) | copy-start | bytes 3076
  50.2 22.7 %copy-start.30 = (f32[32,8]{1,0:T(8,128)}, f32[32,8]{1,0:T(8,128)S(1)}, u32[]{:S(2)}) copy-start(f32[32,8]{1,0:T(8,128)S(1)} %get-tuple-element.39) | copy-start | bytes 3076
  51.5 22.2 %copy-start.26 = (f32[32,8]{1,0:T(8,128)}, f32[32,8]{1,0:T(8,128)S(1)}, u32[]{:S(2)}) copy-start(f32[32,8]{1,0:T(8,128)S(1)} %get-tuple-element.41) | copy-start | bytes 3076
  57.5 4.9 %copy-start.19 = (bf16[32,8,8,128]{3,2,1,0:T(8,128)(2,1)S(1)}, bf16[32,8,8,128]{3,2,1,0:T(8,128)(2,1)}, u32[]{:S(2)}) copy-start(bf16[32,8,8,128]{3,2,1,0:T(8,128)(2,1)} %reshape_reshape_squeeze.7) | copy-start | bytes 1572868
  59.7 19.8 %copy-start.36 = (f32[32,8]{1,0:T(8,128)}, f32[32,8]{1,0:T(8,128)S(1)}, u32[]{:S(2)}) copy-start(f32[32,8]{1,0:T(8,128)S(1)} %get-tuple-element.17) | copy-start | bytes 3076
  66.4 3.8 %copy-start.17 = (f32[32,8,1024]{2,1,0:T(8,128)S(1)}, f32[32,8,1024]{2,1,0:T(8,128)}, u32[]{:S(2)}) copy-start(f32[32,8,1024]{2,1,0:T(8,128)} %get-tuple-element.34) | copy-start | bytes 3145732
  67.7 2.9 %copy-start.21 = (bf16[1,1024,1024]{1,2,0:T(8,128)(2,1)S(1)}, bf16[1,1024,1024]{1,2,0:T(8,128)(2,1)}, u32[]{:S(2)}) copy-start(bf16[1,1024,1024]{1,2,0:T(8,128)(2,1)} %copy.349) | copy-start | bytes 6291460
  76.1 3.4 %copy-start.49 = (f32[32,8]{1,0:T(8,128)}, f32[32,8]{1,0:T(8,128)S(1)}, u32[]{:S(2)}) copy-start(f32[32,8]{1,0:T(8,128)S(1)} %fusion.67) | copy-start | bytes 3076
  76.1 3.4 %copy-start.9 = (f32[32,8,1024]{2,1,0:T(8,128)S(1)}, f32[32,8,1024]{2,1,0:T(8,128)}, u32[]{:S(2)}) copy-start(f32[32,8,1024]{2,1,0:T(8,128)} %get-tuple-element.18) | copy-start | bytes 3145732
  77.5 4.9 %copy-start.8 = (f32[32,8,1024]{2,1,0:T(8,128)S(1)}, f32[32,8,1024]{2,1,0:T(8,128)}, u32[]{:S(2)}) copy-start(f32[32,8,1024]{2,1,0:T(8,128)} %get-tuple-element.20) | copy-start | bytes 3145732
  79.5 3.1 %copy-start.20 = (bf16[1,1024,1024]{1,2,0:T(8,128)(2,1)S(1)}, bf16[1,1024,1024]{1,2,0:T(8,128)(2,1)}, u32[]{:S(2)}) copy-start(bf16[1,1024,1024]{1,2,0:T(8,128)(2,1)} %copy.358) | copy-start | bytes 6291460
  87.9 6.6 %copy-start.22 = (bf16[16,1,2,8192]{3,2,0,1:T(2,128)(2,1)S(1)}, bf16[16,1,2,8192]{3,2,0,1:T(2,128)(2,1)}, u32[]{:S(2)}) copy-start(bf16[16,1,2,8192]{3,2,0,1:T(2,128)(2,1)} %stack_reshape_reshape.14) | copy-start | bytes 1572868
  89.7 9.8 %all-to-all-start.1 = ((f32[16,1,256]{2,1,0:T(1,128)}), f32[16,1,256]{2,1,0:T(1,128)S(1)}, u32[]{:S(2)}, u32[]{:S(2)}) async-start(f32[16,1,256]{2,1,0:T(1,128)} %reshape.539), calls=%async_computation.1 | async-start | bytes 32768 | tf_op jit(solution)/shard_map/all_to_all | solution.py:152
  96.0 8.6 %copy-start.52 = (s32[16]{0:T(128)S(1)}, s32[16]{0:T(128)}, u32[]{:S(2)}) copy-start(s32[16]{0:T(128)} %param.10) | copy-start | bytes 196
  96.0 8.6 %copy-start.24 = (bf16[2,8,64,128]{3,2,1,0:T(8,128)(2,1)S(1)}, bf16[2,8,64,128]{3,2,1,0:T(8,128)(2,1)}, u32[]{:S(2)}) copy-start(bf16[2,8,64,128]{3,2,1,0:T(8,128)(2,1)} %copy.369) | copy-start | bytes 786436
  97.8 9.3 %copy-start.53 = (s32[32,1]{0,1:T(1,128)S(1)}, s32[32,1]{0,1:T(1,128)}, u32[]{:S(2)}) copy-start(s32[32,1]{0,1:T(1,128)} %add.345) | copy-start | bytes 388
  99.5 30.0 %all-to-all-start.2 = ((bf16[16,2,2,8192]{3,2,1,0:T(2,128)(2,1)}), bf16[16,2,2,8192]{3,2,1,0:T(2,128)(2,1)S(1)}, u32[]{:S(2)}, u32[]{:S(2)}) async-start(bf16[16,2,2,8192]{3,2,1,0:T(2,128)(2,1)} %copy.312), calls=%async_computation.2 | async-start | bytes 2097152 | tf_op jit(solution)/shard_map/all_to_all | solution.py:151
  107.0 3.3 %copy-start.51 = (pred[16,2]{1,0:T(8,128)(4,1)S(1)}, pred[16,2]{1,0:T(8,128)(4,1)}, u32[]{:S(2)}) copy-start(pred[16,2]{1,0:T(8,128)(4,1)} %copy.249) | copy-start | bytes 100
  (33 other events, 39.9 us)
where the time goes:
time: 135 us; the launch traced here: 134 us
  local copies, waits for them, and re-layouts  42.3 us (31%)
  matrix products  37 us (27%)
  waiting for transfers between devices  23.4 us (17%)
  starting transfers between devices  16.4 us (12%)
  other arithmetic  13.6 us (10%)
    dot_general x16, matrix products, span_terms(): jnp.einsum('rgd,td->rgt', query_heads[:, kv_head], key_heads[:, kv_head],...  25.1 us
    all_to_all x1, waiting for transfers between devices, body(): lax.all_to_all(part_out, 'owner', split_axis=0, concat_axis=0, tiled=True)  18.9 us
    unnamed x116, local copies, waits for them, and re-layouts  15.1 us
    dot_general x16, matrix products, span_terms(): jnp.einsum('rgt,td->rgd', weights, value_heads[:, kv_head], preferred_ele...  7.25 us
    all_to_all x1, starting transfers between devices, body(): lax.all_to_all(outgoing, 'owner', split_axis=0, concat_axis=0, tiled=True)  6.58 us
    all_to_all x1, starting transfers between devices, body(): lax.all_to_all(part_out, 'owner', split_axis=0, concat_axis=0, tiled=True)  5.04 us
    reduce_sum x16, other arithmetic, span_terms(): summed = jnp.sum(expon, axis=-1)  4.77 us
    all_to_all x1, starting transfers between devices, body(): lax.all_to_all(part_lse, 'owner', split_axis=0, concat_axis=0, tiled=True)  4.76 us
  transfers between devices with their start and end apart: 3, of which 3 were waited for; matrix products, arithmetic and copies ran while one was open for 24% of the time, Pallas kernels for 0%

commit v1 on v0

v1 whole, which is shorter than its diff:
```python
import functools
import math

import jax
import jax.numpy as jnp
from jax import lax
from jax.experimental import pallas as pl
from jax.experimental.pallas import tpu as pltpu
from jax.sharding import PartitionSpec as P

HEADS = 64
KV_HEADS = 8
HEAD_DIM = 128
PREFIXES = 16
CAP = 2

GROUP = HEADS // KV_HEADS
PAIRS = KV_HEADS // 2
FACTOR = 1.0 / math.sqrt(HEAD_DIM)
NEG_FILL = -1e30

BF16 = jnp.bfloat16
F32 = jnp.float32
I32 = jnp.int32

VMEM = pl.BlockSpec(memory_space=pltpu.VMEM)
SMEM = pl.BlockSpec(memory_space=pltpu.SMEM)
ANY = pl.BlockSpec(memory_space=pl.ANY)


def split_pair(tile):
    rows = tile.shape[0]
    wide = tile.astype(F32)
    return [
        wide[:, half * GROUP : (half + 1) * GROUP].reshape(rows * GROUP, HEAD_DIM).astype(BF16)
        for half in range(2)
    ]


def next_cells(prefix_ref, map_ref, count_ref, request, per_prefix, local_slots):
    prefix = prefix_ref[request]
    rank = jnp.minimum(count_ref[prefix], CAP - 1)
    count_ref[prefix] = rank + 1
    cells = []
    for span in range(per_prefix):
        slot = map_ref[prefix * per_prefix + span]
        cells.append((slot // local_slots, (slot % local_slots) * CAP + rank))
    return cells


def clear_counts(count_ref):
    for prefix in range(PREFIXES):
        count_ref[prefix] = 0


def route_kernel(
    per_prefix, local_slots, prefix_ref, map_ref, query_ref, out_ref, rows_ref, stage_ref, count_ref
):
    requests = query_ref.shape[0]
    for head in range(HEADS):
        stage_ref[head * requests : (head + 1) * requests, :] = query_ref[
            :, head * HEAD_DIM : (head + 1) * HEAD_DIM
        ].astype(F32)
    out_ref[...] = jnp.zeros_like(out_ref)
    clear_counts(count_ref)
    for request in range(requests):
        row = stage_ref[pl.ds(request, HEADS, stride=requests), :].astype(BF16)
        rows_ref[request] = row
        for owner, cell in next_cells(
            prefix_ref, map_ref, count_ref, request, per_prefix, local_slots
        ):
            out_ref[owner, cell] = row


def route(queries, prefix, block_map, owners, local_slots):
    requests = queries.shape[0]
    cells = local_slots * CAP
    return pl.pallas_call(
        functools.partial(route_kernel, block_map.shape[0] // PREFIXES, local_slots),
        out_shape=(
            jax.ShapeDtypeStruct((owners, cells, HEADS, HEAD_DIM), BF16),
            jax.ShapeDtypeStruct((requests, HEADS, HEAD_DIM), BF16),
        ),
        in_specs=[SMEM, SMEM, VMEM],
        out_specs=(VMEM, VMEM),
        scratch_shapes=[
            pltpu.VMEM((HEADS * requests, HEAD_DIM), F32),
            pltpu.SMEM((PREFIXES,), I32),
        ],
        name="route",
    )(prefix, block_map, queries)


def span_kernel(rows_ref, key_hbm, value_hbm, out_ref, keys, values, lse_ref, key_sem, value_sem):
    sources, cells = rows_ref.shape[0], rows_ref.shape[1]
    local_slots = key_hbm.shape[0]
    width = 2 * HEAD_DIM
    steps = local_slots * PAIRS

    def fetch(step):
        slot, pair = step // PAIRS, step % PAIRS
        lanes = pl.ds(pair * width, width)
        return (
            pltpu.make_async_copy(key_hbm.at[slot, :, lanes], keys.at[step], key_sem.at[step]),
            pltpu.make_async_copy(value_hbm.at[slot, :, lanes], values.at[step], value_sem.at[step]),
        )

    for step in range(steps):
        for copy in fetch(step):
            copy.start()

    lane = lax.broadcasted_iota(I32, (sources, GROUP, HEAD_DIM), 2)
    room = cells * KV_HEADS
    place = lax.rem(lane, room)
    lse_ref[...] = jnp.zeros_like(lse_ref)

    for step in range(steps):
        slot, pair = step // PAIRS, step % PAIRS
        tile = rows_ref[:, slot * CAP : (slot + 1) * CAP, pair * 2 * GROUP : (pair + 1) * 2 * GROUP, :]
        queries = split_pair(tile.reshape(sources * CAP, 2 * GROUP, HEAD_DIM))
        for copy in fetch(step):
            copy.wait()
        mixed_pair = []
        for half in range(2):
            lanes = slice(half * HEAD_DIM, (half + 1) * HEAD_DIM)
            scores = lax.dot_general(
                queries[half], keys[step, :, lanes], (((1,), (1,)), ((), ())), preferred_element_type=F32
            )
            highest = jnp.max(scores, axis=1, keepdims=True)
            expon = jnp.exp((scores - highest) * FACTOR)
            summed = jnp.sum(expon, axis=1, keepdims=True)
            mixed = jnp.dot(expon.astype(BF16), values[step, :, lanes], preferred_element_type=F32)
            mixed_pair.append((mixed / summed).reshape(sources, CAP, GROUP, HEAD_DIM))
            lse = jnp.broadcast_to(highest * FACTOR + jnp.log(summed), (sources * CAP * GROUP, HEAD_DIM))
            lse = lse.reshape(sources, CAP, GROUP, HEAD_DIM)
            kv_head = pair * 2 + half
            for cap in range(CAP):
                at = (slot * CAP + cap) * KV_HEADS + kv_head
                lse_ref[...] = jnp.where(place == at, lse[:, cap], lse_ref[...])
        both = jnp.concatenate(mixed_pair, axis=2).astype(BF16)
        for cap in range(CAP):
            start = (slot * CAP + cap) * HEADS + pair * 2 * GROUP
            out_ref[:, start : start + 2 * GROUP, :] = both[:, cap]

    lse = lse_ref[...]
    high = lse.astype(BF16).astype(F32)
    middle = (lse - high).astype(BF16).astype(F32)
    low = lse - high - middle
    pieces = jnp.where(lane < room, high, jnp.where(lane < 2 * room, middle, low))
    pieces = jnp.concatenate([pieces, jnp.zeros_like(pieces)], axis=1).astype(BF16)
    out_ref[:, cells * HEADS : cells * HEADS + 2 * GROUP, :] = pieces


def spans(rows, prefix_keys, prefix_values):
    sources, cells = rows.shape[0], rows.shape[1]
    local_slots, tokens = prefix_keys.shape[0], prefix_keys.shape[1]
    steps = local_slots * PAIRS
    area = sources * cells * HEADS * tokens
    return pl.pallas_call(
        span_kernel,
        out_shape=jax.ShapeDtypeStruct((sources, cells * HEADS + 2 * GROUP, HEAD_DIM), BF16),
        in_specs=[VMEM, ANY, ANY],
        out_specs=VMEM,
        scratch_shapes=[
            pltpu.VMEM((steps, tokens, 2 * HEAD_DIM), BF16),
            pltpu.VMEM((steps, tokens, 2 * HEAD_DIM), BF16),
            pltpu.VMEM((sources, GROUP, HEAD_DIM), F32),
            pltpu.SemaphoreType.DMA((steps,)),
            pltpu.SemaphoreType.DMA((steps,)),
        ],
        compiler_params=pltpu.CompilerParams(vmem_limit_bytes=56 << 20),
        cost_estimate=pl.CostEstimate(
            flops=4 * area * HEAD_DIM,
            transcendentals=area,
            bytes_accessed=4 * prefix_keys.size + 4 * rows.size,
        ),
        name="spans",
    )(rows, prefix_keys, prefix_values)


def suffix_kernel(len_ref, query_ref, key_ref, value_ref, out_ref, lse_out_ref, bias_ref):
    requests, room = key_ref.shape[0], key_ref.shape[1]
    column = lax.broadcasted_iota(I32, (GROUP, requests * room), 1)
    for request in range(requests):
        first = request * room
        seen = (column >= first) & (column < first + len_ref[request])
        bias_ref[request * GROUP : (request + 1) * GROUP, :] = jnp.where(seen, 0.0, NEG_FILL)
    lane = lax.broadcasted_iota(I32, (requests, GROUP, HEAD_DIM), 2)
    lse_all = jnp.zeros((requests, GROUP, HEAD_DIM), F32)
    for pair in range(PAIRS):
        queries = split_pair(query_ref[:, pair * 2 * GROUP : (pair + 1) * 2 * GROUP, :])
        for half in range(2):
            kv_head = pair * 2 + half
            lanes = slice(kv_head * HEAD_DIM, (kv_head + 1) * HEAD_DIM)
            key_rows = key_ref[:, :, lanes].reshape(requests * room, HEAD_DIM)
            value_rows = value_ref[:, :, lanes].reshape(requests * room, HEAD_DIM)
            scores = lax.dot_general(
                queries[half], key_rows, (((1,), (1,)), ((), ())), preferred_element_type=F32
            )
            scores = jnp.where(bias_ref[...] < 0.0, NEG_FILL, scores)
            highest = jnp.max(scores, axis=1, keepdims=True)
            expon = jnp.exp((scores - highest) * FACTOR)
            summed = jnp.sum(expon, axis=1, keepdims=True)
            mixed = jnp.dot(expon.astype(BF16), value_rows, preferred_element_type=F32)
            out_ref[:, kv_head * GROUP : (kv_head + 1) * GROUP, :] = (mixed / summed).reshape(
                requests, GROUP, HEAD_DIM
            )
            lse = jnp.broadcast_to(highest * FACTOR + jnp.log(summed), (requests * GROUP, HEAD_DIM))
            lse_all = jnp.where(lane == kv_head, lse.reshape(requests, GROUP, HEAD_DIM), lse_all)
    lse_out_ref[...] = lse_all


def suffixes(rows, suffix_len, suffix_keys, suffix_values):
    requests, room = suffix_keys.shape[0], suffix_keys.shape[1]
    return pl.pallas_call(
        suffix_kernel,
        out_shape=(
            jax.ShapeDtypeStruct((requests, HEADS, HEAD_DIM), F32),
            jax.ShapeDtypeStruct((requests, GROUP, HEAD_DIM), F32),
        ),
        in_specs=[SMEM, VMEM, VMEM, VMEM],
        out_specs=(VMEM, VMEM),
        scratch_shapes=[pltpu.VMEM((requests * GROUP, requests * room), F32)],
        cost_estimate=pl.CostEstimate(
            flops=4 * requests * HEADS * requests * room * HEAD_DIM,
            transcendentals=requests * HEADS * requests * room,
            bytes_accessed=4 * suffix_keys.size + 6 * rows.size,
        ),
        name="suffixes",
    )(suffix_len, rows, suffix_keys, suffix_values)


def combine_kernel(
    per_prefix,
    local_slots,
    prefix_ref,
    map_ref,
    back_ref,
    suffix_ref,
    suffix_lse_ref,
    out_ref,
    stage_ref,
    count_ref,
):
    requests = out_ref.shape[0]
    cells = local_slots * CAP
    room = cells * KV_HEADS
    clear_counts(count_ref)
    for request in range(requests):
        places = next_cells(prefix_ref, map_ref, count_ref, request, per_prefix, local_slots)
        lses = []
        for owner, cell in places:
            pieces = back_ref[owner, cells * HEADS : cells * HEADS + 2 * GROUP, :].astype(F32)[:GROUP]
            pieces = pltpu.roll(pieces, lax.rem(HEAD_DIM - cell * KV_HEADS, HEAD_DIM), 1)
            lses.append(
                pieces
                + pltpu.roll(pieces, HEAD_DIM - room, 1)
                + pltpu.roll(pieces, HEAD_DIM - 2 * room, 1)
            )
        lses.append(suffix_lse_ref[request])
        top = functools.reduce(jnp.maximum, lses)
        scales = [jnp.exp(lse - top) for lse in lses]
        total = functools.reduce(jnp.add, scales)
        weights = [scale / total for scale in scales]
        for pair in range(PAIRS):
            parts = []
            for owner, cell in places:
                start = pl.multiple_of(cell * HEADS + pair * 2 * GROUP, 2 * GROUP)
                parts.append(back_ref[owner, pl.ds(start, 2 * GROUP), :].astype(F32))
            parts.append(suffix_ref[request, pair * 2 * GROUP : (pair + 1) * 2 * GROUP, :])
            for half in range(2):
                kv_head = pair * 2 + half
                mixed = functools.reduce(
                    jnp.add,
                    [
                        weight[:, kv_head : kv_head + 1] * part[half * GROUP : (half + 1) * GROUP]
                        for weight, part in zip(weights, parts)
                    ],
                )
                stage_ref[pl.ds(kv_head * GROUP * requests + request, GROUP, stride=requests), :] = mixed
    for head in range(HEADS):
        out_ref[:, head * HEAD_DIM : (head + 1) * HEAD_DIM] = stage_ref[
            head * requests : (head + 1) * requests, :
        ].astype(BF16)


def combine(back, prefix, block_map, suffix_out, suffix_lse, local_slots):
    requests = suffix_out.shape[0]
    return pl.pallas_call(
        functools.partial(combine_kernel, block_map.shape[0] // PREFIXES, local_slots),
        out_shape=jax.ShapeDtypeStruct((requests, HEADS * HEAD_DIM), BF16),
        in_specs=[SMEM, SMEM, VMEM, VMEM, VMEM],
        out_specs=VMEM,
        scratch_shapes=[
            pltpu.VMEM((HEADS * requests, HEAD_DIM), F32),
            pltpu.SMEM((PREFIXES,), I32),
        ],
        name="combine",
    )(prefix, block_map, back, suffix_out, suffix_lse)


def exchange(blocks):
    return lax.all_to_all(blocks, "owner", split_axis=0, concat_axis=0, tiled=True)


def body(
    queries,
    request_prefix,
    suffix_len,
    block_map,
    prefix_keys,
    prefix_values,
    suffix_keys,
    suffix_values,
):
    owners = lax.axis_size("owner")
    local_slots = prefix_keys.shape[0]
    prefix = request_prefix[:, 0]
    outgoing, rows = route(queries, prefix, block_map, owners, local_slots)
    received = exchange(outgoing)
    suffix_out, suffix_lse = suffixes(rows, suffix_len, suffix_keys, suffix_values)
    back = exchange(spans(received, prefix_keys, prefix_values))
    return combine(back, prefix, block_map, suffix_out, suffix_lse, local_slots)


def solution(mesh):
    placed = (
        P(("groups", "owner"), None),
        P(("groups", "owner"), None),
        P(("groups", "owner")),
        P("groups"),
        P(("groups", "owner"), None, None),
        P(("groups", "owner"), None, None),
        P(("groups", "owner"), None, None),
        P(("groups", "owner"), None, None),
    )
    return jax.shard_map(
        body, mesh=mesh, in_specs=placed, out_specs=P(("groups", "owner"), None), check_vma=False
    )
```

time: 135 us -> 84.6 us (0.63)
  local copies, waits for them, and re-layouts: 42.3 us -> 0.99 us
  matrix products: 37 us -> 0 us
  blocking collectives: 0 us -> 32 us
  Pallas kernels: 0 us -> 25.3 us
  other arithmetic: 13.6 us -> 0 us
  starting transfers between devices: 16.4 us -> 4.37 us
  waiting for transfers between devices: 23.4 us -> 21.5 us
    dot_general x35 -> x0, matrix products: 37 us -> none  [the longest x16 25.1 us: span_terms(): jnp.einsum('rgd,td->rgt', query_heads[:, kv_head], key_heads[:, kv_head],...]
    all_to_all x0 -> x1, blocking collectives: none -> 32 us  [exchange(): lax.all_to_all(blocks, 'owner', split_axis=0, concat_axis=0, tiled=True)]
    pallas_call x0 -> x4, Pallas kernels: none -> 25.3 us  [the longest x1 13 us: spans(): pl.pallas_call(span_kernel, out_shape=jax.ShapeDtypeStruct((sources, cell...]
    unnamed x116 -> x2, local copies, waits for them, and re-layouts: 15.1 us -> 0.99 us
    all_to_all x3 -> x1, starting transfers between devices: 16.4 us -> 4.37 us  [exchange(): lax.all_to_all(blocks, 'owner', split_axis=0, concat_axis=0, tiled=True)]
    slice x3 -> x0, local copies, waits for them, and re-layouts: 11.5 us -> none  [the longest x1 4.01 us: attend_rows(): prefix_keys[slot_index]]
    another operation x12 -> x0, local copies, waits for them, and re-layouts: 9.97 us -> none  [the longest x2 4.47 us: span_terms(): query_heads = rows.reshape(row_count, KV_HEADS, per_group, HEAD_DIM)]
    reduce_sum x21 -> x0, other arithmetic: 7.45 us -> none  [the longest x16 4.77 us: span_terms(): summed = jnp.sum(expon, axis=-1)]
  transfers between devices with their start and end apart: 3 -> 1, of which waited for: 3 -> 1; matrix products, arithmetic and copies ran while one was open for 24% -> 0% of each run, Pallas kernels for 0% -> 6%
where the time goes in v1:
time: 84.6 us; the launch traced here: 84.2 us
  blocking collectives  32 us (38%)
  Pallas kernels  25.3 us (30%)
  waiting for transfers between devices  21.5 us (25%)
  starting transfers between devices  4.37 us (5%)
  local copies, waits for them, and re-layouts  0.99 us (1%)
    all_to_all x1, blocking collectives, exchange(): lax.all_to_all(blocks, 'owner', split_axis=0, concat_axis=0, tiled=True)  32 us
    all_to_all x1, waiting for transfers between devices, exchange(): lax.all_to_all(blocks, 'owner', split_axis=0, concat_axis=0, tiled=True)  21.5 us
    pallas_call x1, Pallas kernels, spans(): pl.pallas_call(span_kernel, out_shape=jax.ShapeDtypeStruct((sources, cell...  13 us
    pallas_call x1, Pallas kernels, combine(): pl.pallas_call(functools.partial(combine_kernel, block_map.shape[0] // PR...  5.12 us
    pallas_call x1, Pallas kernels, suffixes(): pl.pallas_call(suffix_kernel, out_shape=(jax.ShapeDtypeStruct((requests,...  4.75 us
    all_to_all x1, starting transfers between devices, exchange(): lax.all_to_all(blocks, 'owner', split_axis=0, concat_axis=0, tiled=True)  4.37 us
    pallas_call x1, Pallas kernels, route(): pl.pallas_call(functools.partial(route_kernel, block_map.shape[0] // PREF...  2.46 us
  transfers between devices with their start and end apart: 1, of which 1 were waited for; matrix products, arithmetic and copies ran while one was open for 0% of the time, Pallas kernels for 6%

profile of v1, /device:TPU:9, one launch (start us, length us, event | category | flops | bytes accessed | tf_op | source)
XLA Modules:
  0.0 84.2 jit_solution(1355310761870690585)
XLA Ops:
  0.0 2.5 %route.1 = (bf16[16,4,64,128]{3,2,1,0:T(8,128)(2,1)}, bf16[16,64,128]{2,1,0:T(8,128)(2,1)}) custom-call(s32[16]{0:T(128)} %bitcast.1, s32[32]{0:T(128)} %map_ref.3, bf16[16,8192]{1,0:T(8,128)(2,1)} %query_ref.1), custom_call_target="tpu_custom_call" | custom-call | tf_op jit(solution)/shard_map/route/pallas_call | solution.py:78
  2.5 32.0 %all_to_all.10.rows_ref = bf16[16,4,64,128]{3,2,1,0:T(8,128)(2,1)} all-to-all(bf16[16,4,64,128]{3,2,1,0:T(8,128)(2,1)} %get-tuple-element.9), channel_id=1, replica_groups=mesh['groups'=2,'owner'=16] {'owner'}, dimensions={0} | all-to-all | bytes 2097152 | tf_op jit(solution)/shard_map/all_to_all | solution.py:303
  34.5 13.0 %spans.1 = bf16[16,272,128]{2,1,0:T(8,128)(2,1)} custom-call(bf16[16,4,64,128]{3,2,1,0:T(8,128)(2,1)} %all_to_all.10.rows_ref, bf16[2,1024,1024]{2,1,0:T(8,128)(2,1)} %key_hbm.1, bf16[2,1024,1024]{2,1,0:T(8,128)(2,1)} %value_hbm.1), custom_call_target="tpu_custom_call" | custom-call | flops 2147483648 | bytes 10485760 | tf_op jit(solution)/shard_map/spans/pallas_call | solution.py:159
  47.5 4.4 %all-to-all-start.1 = ((bf16[16,272,128]{2,1,0:T(8,128)(2,1)}), bf16[16,272,128]{2,1,0:T(8,128)(2,1)S(1)}, u32[]{:S(2)}, u32[]{:S(2)}) async-start(bf16[16,272,128]{2,1,0:T(8,128)(2,1)} %spans.1), calls=%async_computation.1 | async-start | bytes 2228224 | tf_op jit(solution)/shard_map/all_to_all | solution.py:303
  51.9 4.8 %suffixes.1 = (f32[16,64,128]{2,1,0:T(8,128)}, f32[16,8,128]{2,1,0:T(8,128)}) custom-call(s32[16]{0:T(128)} %len_ref.1, bf16[16,64,128]{2,1,0:T(8,128)(2,1)} %get-tuple-element.10.query_ref, bf16[16,32,1024]{2,1,0:T(8,128)(2,1)} %key_ref.1, bf16[16,32,1024]{2,1,0:T(8,128)(2,1)} %value_ref.1), custom_call_target="tpu_custom_call" | custom-call | flops 268435456 | bytes 2883584 | tf_op jit(solution)/shard_map/suffixes/pallas_call | solution.py:215
  56.6 21.5 %all-to-all-done.1.back_ref = bf16[16,272,128]{2,1,0:T(8,128)(2,1)S(1)} async-done(((bf16[16,272,128]{2,1,0:T(8,128)(2,1)}), bf16[16,272,128]{2,1,0:T(8,128)(2,1)S(1)}, u32[]{:S(2)}, u32[]{:S(2)}) %all-to-all-start.1) | async-done | bytes 1114144 | tf_op jit(solution)/shard_map/all_to_all | solution.py:303
  78.1 0.0 copy-start
  78.1 1.0 %copy-done = bf16[16,272,128]{2,1,0:T(8,128)(2,1)} copy-done((bf16[16,272,128]{2,1,0:T(8,128)(2,1)}, bf16[16,272,128]{2,1,0:T(8,128)(2,1)S(1)}, u32[]{:S(2)}) %copy-start) | copy-done | bytes 1114136
  79.1 5.1 %combine.1 = bf16[16,8192]{1,0:T(8,128)(2,1)} custom-call(s32[16]{0:T(128)} %bitcast.2, s32[32]{0:T(128)} %map_ref.3, bf16[16,272,128]{2,1,0:T(8,128)(2,1)} %copy-done, f32[16,64,128]{2,1,0:T(8,128)} %get-tuple-element.11.suffix_ref, f32[16,8,128]{2,1,0:T(8,128)} %get-tuple-element.12.suffix_lse_ref), custom_call_target="tpu_custom_call" | custom-call | tf_op jit(solution)/shard_map/combine/pallas_call | solution.py:289
Async XLA Ops:
  47.5 30.6 %all-to-all-start.1 = ((bf16[16,272,128]{2,1,0:T(8,128)(2,1)}), bf16[16,272,128]{2,1,0:T(8,128)(2,1)S(1)}, u32[]{:S(2)}, u32[]{:S(2)}) async-start(bf16[16,272,128]{2,1,0:T(8,128)(2,1)} %spans.1), calls=%async_computation.1 | async-start | bytes 2228224 | tf_op jit(solution)/shard_map/all_to_all | solution.py:303
  78.1 1.0 %copy-start = (bf16[16,272,128]{2,1,0:T(8,128)(2,1)}, bf16[16,272,128]{2,1,0:T(8,128)(2,1)S(1)}, u32[]{:S(2)}) copy-start(bf16[16,272,128]{2,1,0:T(8,128)(2,1)S(1)} %all-to-all-done.1.back_ref) | copy-start | bytes 3342340
